TPU v7x, 128 devices: a whole 4x4x4 slice. The times are simulated.
128 devices in a mesh: seq: 8 (over x, y_hi), fsdp: 16 (over y_lo, z, core).
Axes of the slice: x: 4, y: 4 (y_hi: 2, y_lo: 2; y = y_hi * 2 + y_lo), z: 4, core: 2. Of those that a mesh axis runs over, the one named last changes fastest.
Arguments:
- patches: bfloat16 [16, 2048, 1152], P('fsdp'), may hold values from -6 to 6
- counts: int32 [16, 8], P('fsdp'), may hold values from 1 to 505, as said below
- starts: int32 [16, 8], P('fsdp'), may hold values from 0 to 1023, as said below
- embeds: bfloat16 [16, 1024, 2048], P('fsdp', 'seq'), may hold values from -6 to 6
- route_ids: int32 [16, 1024, 6], P('fsdp'), may hold values from 0 to 63, all different within a row; in each aligned block of 1024 rows (0 to 1023, 1024 to 2047, ..., all dimensions but the last counted through in order) at most 128 rows name the same one
- route_weights: float32 [16, 1024, 6], P('fsdp'), may hold values from 0.1 to 0.6
- vit_gain: float32 [1152], replicated, may hold values from 0.5 to 1.5
- vit_fc1: bfloat16 [1152, 4304], P('fsdp', 'seq'), may hold values from -0.1875 to 0.1875
- vit_fc2: bfloat16 [1152, 4304], P('fsdp', 'seq'), may hold values from -0.09375 to 0.09375
- proj_gain: float32 [4608], replicated, may hold values from 0.5 to 1.5
- proj_weight: bfloat16 [4608, 2048], P('fsdp', 'seq'), may hold values from -0.09375 to 0.09375
- moe_gain: float32 [2048], replicated, may hold values from 0.5 to 1.5
- shared_gate: bfloat16 [2048, 2816], P('fsdp', 'seq'), may hold values from -0.125 to 0.125
- shared_up: bfloat16 [2048, 2816], P('fsdp', 'seq'), may hold values from -0.125 to 0.125
- shared_down: bfloat16 [2048, 2816], P('fsdp', 'seq'), may hold values from -0.109375 to 0.109375
- expert_gate: bfloat16 [2048, 8, 1408], P('fsdp', 'seq'), may hold values from -0.125 to 0.125
- expert_up: bfloat16 [2048, 8, 1408], P('fsdp', 'seq'), may hold values from -0.125 to 0.125
- expert_down: bfloat16 [2048, 8, 1408], P('fsdp', 'seq'), may hold values from -0.15625 to 0.15625
Outputs:
- layer_out: bfloat16 [16, 1024, 2048], P('fsdp', 'seq')
Inputs may be any that keep to these rules, and one draw needn't show every extreme that they name: Per stream the counts of its 8 images sum to 512. `starts`: images of a stream lie in order in disjoint runs of positions inside its 1024 positions; in each stream the 128 positions of some one index of seq are all visual. `route_ids`: the 6 experts of a token differ; in each stream no expert is chosen by more than 128 tokens.
All inputs are finite; a program needn't handle non-finite values.
Results may differ from a plain program's by a relative error of at most 0.014.
Values may be sent and summed in bfloat16 or wider, within the bound.
No kernel may reach another device: no remote copies, remote signals or barrier semaphores. Data moves between devices by JAX's collectives and lax.ppermute only.
A program may use at most 128 MiB of HBM per device.

v0:
```python
import jax
import jax.numpy as jnp
from jax import lax
from jax.sharding import PartitionSpec as P

ln_epsilon = 1e-05
rms_epsilon = 1e-06


def sent_together(arrays, axis, dim, along):
    both = jnp.concatenate(arrays, axis=along)
    result, at, gathered = (lax.all_gather(both, axis, axis=dim, tiled=True), 0, [])
    for a in arrays:
        gathered.append(lax.slice_in_dim(result, at, at + a.shape[along], axis=along))
        at += a.shape[along]
    return tuple(gathered)


def rows_for(lines, count):
    spare = -len(lines) % count
    return jnp.pad(lines, [(0, spare)] + [(0, 0)] * (lines.ndim - 1))


def sum_in_two_steps(x, axis):
    lines = x.reshape(-1, *x.shape[1:][-1:])
    own = lax.psum_scatter(
        rows_for(lines, lax.axis_size(axis)), axis, scatter_dimension=0, tiled=True
    )
    whole = lax.all_gather(own, axis).reshape(-1, *lines.shape[1:])
    return lax.slice_in_dim(whole, 0, len(lines)).reshape(x.shape)


def in_one_piece(arrays, axis, dim, along):
    columns = [a.reshape(*a.shape[:along], -1) for a in arrays]
    both = jnp.concatenate(columns, axis=along)
    result, at, gathered = (lax.all_gather(both, axis, axis=dim, tiled=True), 0, [])
    for a, column in zip(arrays, columns):
        piece = result[..., at : at + column.shape[along]]
        gathered.append(piece.reshape(*piece.shape[:along], *a.shape[along:]))
        at += column.shape[along]
    return tuple(gathered)


def split_up(x, dim, count):
    shape = x.shape
    parts = x.reshape(*shape[:dim], count, shape[dim] // count, *shape[dim + 1 :])
    return jnp.moveaxis(parts, dim, 0)


def sum_at_owner(x, axis, dim):
    count = lax.axis_size(axis)
    parts = lax.all_to_all(split_up(x, dim, count), axis, 0, 0, tiled=True)
    return jnp.sum(parts.astype(jnp.float32), axis=0)


def layer_norm(values, gain_vec):
    center = values - jnp.mean(values, axis=-1, keepdims=True)
    spread = jnp.mean(center * center, axis=-1, keepdims=True)
    return center * lax.rsqrt(spread + ln_epsilon) * gain_vec


def rms_norm(values, gain_vec):
    square = jnp.mean(values * values, axis=-1, keepdims=True)
    return values * lax.rsqrt(square + rms_epsilon) * gain_vec


def visual_positions(counts, starts, total):
    end_index = jnp.cumsum(counts)
    begins = end_index - counts
    token_index = jnp.arange(total, dtype=jnp.int32)
    inside = (token_index[:, None] >= begins[None, :]) & (token_index[:, None] < end_index[None, :])
    placed = starts[None, :] + token_index[:, None] - begins[None, :]
    return jnp.sum(jnp.where(inside, placed, 0), axis=1)


def routed_rows(gathered, route_ids, route_weights, expert, capacity, gate_w, up_w, down_w):
    hit_mask = route_ids == expert
    chosen = jnp.any(hit_mask, axis=1)
    weight_sum = jnp.sum(jnp.where(hit_mask, route_weights, 0.0), axis=1)
    count_rows = gathered.shape[0]
    slot_rank = jnp.cumsum(chosen.astype(jnp.int32)) - 1
    target = jnp.where(chosen, slot_rank, capacity)
    slot_rows = (
        jnp.zeros((capacity,), jnp.int32)
        .at[target]
        .set(jnp.arange(count_rows, dtype=jnp.int32), mode="drop")
    )
    is_live = jnp.arange(capacity, dtype=jnp.int32) < jnp.sum(chosen.astype(jnp.int32))
    picked = jnp.take(gathered, slot_rows, axis=0)
    gate_part = jnp.dot(picked, gate_w, preferred_element_type=jnp.float32)
    up_part = jnp.dot(picked, up_w, preferred_element_type=jnp.float32)
    hidden = (jax.nn.silu(gate_part) * up_part).astype(jnp.bfloat16)
    result = lax.dot_general(
        hidden, down_w, (((1,), (1,)), ((), ())), preferred_element_type=jnp.float32
    )
    factor = jnp.where(is_live, jnp.take(weight_sum, slot_rows), 0.0)
    return (slot_rows, result * factor[:, None])


def shards(
    patches,
    counts,
    starts,
    embeds,
    route_ids,
    route_weights,
    vit_gain,
    vit_fc1,
    vit_fc2,
    proj_gain,
    proj_weight,
    moe_gain,
    shared_gate,
    shared_up,
    shared_down,
    expert_gate,
    expert_up,
    expert_down,
):
    seq_count = lax.axis_size("seq")
    seq_index = lax.axis_index("seq")
    vit_first, vit_second, projector = (
        *sent_together((vit_fc1, vit_fc2), "fsdp", 0, 1),
        lax.all_gather(proj_weight, "fsdp", axis=0, tiled=True),
    )
    image_rows = patches[0].astype(jnp.float32)
    normed = layer_norm(image_rows, vit_gain).astype(jnp.bfloat16)
    hidden = jax.nn.gelu(
        jnp.dot(normed, vit_first, preferred_element_type=jnp.float32), approximate=True
    ).astype(jnp.bfloat16)
    product = lax.dot_general(
        hidden, vit_second, (((1,), (1,)), ((), ())), preferred_element_type=jnp.float32
    )
    mixed_sum = sum_in_two_steps(product.astype(jnp.bfloat16), "seq").astype(jnp.float32)
    residual = image_rows + mixed_sum
    joined_width = residual.shape[1] * 4
    proj_in = layer_norm(residual.reshape(-1, joined_width), proj_gain).astype(jnp.bfloat16)
    visual = jnp.dot(proj_in, projector, preferred_element_type=jnp.float32).astype(jnp.bfloat16)
    tok_dev = embeds.shape[1]
    positions = visual_positions(counts[0], starts[0], visual.shape[0])
    owners = positions // tok_dev
    one_hot = (owners[:, None] == jnp.arange(seq_count, dtype=jnp.int32)[None, :]).astype(jnp.int32)
    slot_rank = jnp.sum((jnp.cumsum(one_hot, axis=0) - one_hot) * one_hot, axis=1)
    slot_index = owners * tok_dev + slot_rank
    send_buffer = (
        jnp.zeros((seq_count * tok_dev, visual.shape[1]), jnp.bfloat16).at[slot_index].set(visual)
    )
    received = lax.all_to_all(
        send_buffer.reshape(seq_count, tok_dev, visual.shape[1]),
        "seq",
        split_axis=0,
        concat_axis=2,
        tiled=True,
    )
    is_mine = owners == seq_index
    local_rows = positions % tok_dev
    slot_place = (
        jnp.full((tok_dev,), tok_dev, jnp.int32)
        .at[jnp.where(is_mine, slot_rank, tok_dev)]
        .set(local_rows, mode="drop")
    )
    merged = embeds[0].at[slot_place].set(received[0], mode="drop")
    normed_tokens = rms_norm(merged.astype(jnp.float32), moe_gain).astype(jnp.bfloat16)
    gathered = lax.all_gather(normed_tokens, "seq", axis=0, tiled=True)
    gate_shared, up_shared, down_shared, gate_expert, up_expert, down_expert = in_one_piece(
        (shared_gate, shared_up, shared_down, expert_gate, expert_up, expert_down), "fsdp", 0, 1
    )
    gate_part = jnp.dot(gathered, gate_shared, preferred_element_type=jnp.float32)
    up_part = jnp.dot(gathered, up_shared, preferred_element_type=jnp.float32)
    shared_hidden = (jax.nn.silu(gate_part) * up_part).astype(jnp.bfloat16)
    partial_value = lax.dot_general(
        shared_hidden, down_shared, (((1,), (1,)), ((), ())), preferred_element_type=jnp.float32
    )
    capacity = gathered.shape[0] // 8
    local_count = gate_expert.shape[1]
    expert = seq_index * local_count + 0
    slot_rows, values = routed_rows(
        gathered,
        route_ids[0],
        route_weights[0],
        expert,
        capacity,
        gate_expert[:, 0, :],
        up_expert[:, 0, :],
        down_expert[:, 0, :],
    )
    partial_value = partial_value.at[slot_rows].add(values)
    summed = sum_at_owner(partial_value.astype(jnp.bfloat16), "seq", 0)
    layer_out = (merged.astype(jnp.float32) + summed).astype(jnp.bfloat16)
    return layer_out[None]


def solution(mesh):
    placed = (
        P("fsdp", None, None),
        P("fsdp", None),
        P("fsdp", None),
        P("fsdp", "seq", None),
        P("fsdp", None, None),
        P("fsdp", None, None),
        P(),
        P("fsdp", "seq"),
        P("fsdp", "seq"),
        P(),
        P("fsdp", "seq"),
        P(),
        P("fsdp", "seq"),
        P("fsdp", "seq"),
        P("fsdp", "seq"),
        P("fsdp", "seq", None),
        P("fsdp", "seq", None),
        P("fsdp", "seq", None),
    )
    return jax.shard_map(
        shards, mesh=mesh, in_specs=placed, out_specs=P("fsdp", "seq", None), check_vma=False
    )
```

profile of v0, /device:TPU:0, one launch (start us, length us, event | category | flops | bytes accessed | tf_op | source)
XLA Modules:
  0.0 584.5 jit_solution(8994324096411990108)
XLA Ops:
  6.5 1.7 pad_maximum_fusion
  8.3 3.2 convert_reduce_fusion
  12.1 1.4 multiply_reduce_fusion.1
  13.5 33.0 %all-gather.7.cloned.1.call-done = bf16[1152,1076]{1,0:T(8,128)(2,1)} async-done(((bf16[72,1076]{1,0:T(8,128)(2,1)}), bf16[1152,1076]{1,0:T(8,128)(2,1)}) %all-gather.7.cloned.1.call-update) | async-done | bytes 2479120 | tf_op jit(solution)/shard_map/all_gather | solution.py:12
  46.5 13.0 %convolution_convert_fusion = bf16[2048,1152]{1,0:T(8,128)(2,1)} fusion(bf16[1152,1076]{1,0:T(8,128)(2,1)} %all-gather.7.cloned.1.call-done, bf16[1,2048,1152]{2,1,0:T(8,128)(2,1)} %param.18, f32[1152]{0:T(1024)S(1)} %copy-done.13, f32[2048]{0:T(1024)S(1)} %add_rsqrt_fusion, f32[2048]{0:T(1024)S(1)} %broadcast_multiply_fusion), kind=kOutput, calls=%fused_computation.15 | convolution fusion | flops 5101277184 | bytes 12407296 | tf_op jit(solution)/shard_map/dot_general | solution.py:131
  59.5 88.6 %reduce-scatter.2.cloned.1.call-done = bf16[256,1152]{1,0:T(8,128)(2,1)} async-done(((bf16[2048,1152]{1,0:T(8,128)(2,1)}), bf16[256,1152]{1,0:T(8,128)(2,1)}) %reduce-scatter.2.cloned.1.call-update) | async-done | bytes 589840 | tf_op jit(solution)/shard_map/reduce_scatter | solution.py:26
  148.7 8.6 %reshape.281 = f32[512,4608]{1,0:T(8,128)} reshape(bf16[1,2048,1152]{2,1,0:T(8,128)(2,1)} %param.18) | data formatting | bytes 14155776 | tf_op jit(solution)/shard_map/convert_element_type | solution.py:126
  157.6 1.1 reduce-window.20
  159.2 65.9 %all-gather.15.cloned.1.call-done = bf16[2048,1152]{1,0:T(8,128)(2,1)} async-done(((bf16[256,1152]{1,0:T(8,128)(2,1)}), bf16[2048,1152]{1,0:T(8,128)(2,1)}) %all-gather.15.cloned.1.call-update) | async-done | bytes 4718608 | tf_op jit(solution)/shard_map/all_gather | solution.py:29
  225.0 5.1 fusion
  230.8 5.8 multiply_reduce_fusion
  237.1 8.6 %reshape.282 = f32[512,4608]{1,0:T(8,128)} reshape(bf16[2048,1152]{1,0:T(8,128)(2,1)} %all-gather.15.cloned.1.call-done) | data formatting | bytes 14155776 | tf_op jit(solution)/shard_map/convert_element_type | solution.py:134
  245.7 13.3 %all-gather.9.cloned.1.call-done = bf16[4608,256]{1,0:T(8,128)(2,1)} async-done(((bf16[288,256]{1,0:T(8,128)(2,1)}), bf16[4608,256]{1,0:T(8,128)(2,1)}) %all-gather.9.cloned.1.call-update) | async-done | bytes 2359312 | tf_op jit(solution)/shard_map/all_gather | solution.py:124
  259.0 8.6 %fusion.49 = bf16[512,256]{1,0:T(8,128)(2,1)S(1)} fusion(bf16[4608,256]{1,0:T(8,128)(2,1)} %all-gather.9.cloned.1.call-done, f32[512,4608]{1,0:T(8,128)} %reshape.281, f32[512,4608]{1,0:T(8,128)} %reshape.282, f32[4608]{0:T(1024)S(1)} %copy-done.10, f32[512]{0:T(512)S(1)} %add_rsqrt_fusion.1, f32[512]{0:T(512)S(1)} %broadcast_multiply_fusion.1), kind=kOutput, calls=%fused_computation.53 | convolution fusion | flops 1219887104 | bytes 21518336 | tf_op jit(solution)/shard_map/dot_general | solution.py:138
  267.6 3.1 scatter_custom_fusion.1
  270.7 6.4 %all-to-all-start = ((bf16[8,128,256]{2,1,0:T(8,128)(2,1)}), bf16[8,128,256]{2,1,0:T(8,128)(2,1)S(1)}, u32[]{:S(2)}, u32[]{:S(2)}) async-start(bf16[8,128,256]{2,1,0:T(8,128)(2,1)} %bitcast.15), calls=%async_computation.1 | async-start | bytes 1048576 | tf_op jit(solution)/shard_map/all_to_all | solution.py:148
  277.2 2.4 scatter_custom_fusion
  279.7 8.7 %all-to-all-done = bf16[8,128,256]{2,1,0:T(8,128)(2,1)S(1)} async-done(((bf16[8,128,256]{2,1,0:T(8,128)(2,1)}), bf16[8,128,256]{2,1,0:T(8,128)(2,1)S(1)}, u32[]{:S(2)}, u32[]{:S(2)}) %all-to-all-start) | async-done | bytes 524320 | tf_op jit(solution)/shard_map/all_to_all | solution.py:148
  288.6 1.6 scatter_fusion
  291.9 2.7 concatenate.7
  295.4 4.3 scatter_custom_fusion.3
  299.8 1.1 gather_fusion.1
  302.2 57.9 %all-gather.11.cloned.1.call-done = bf16[1024,2048]{1,0:T(8,128)(2,1)} async-done(((bf16[128,2048]{1,0:T(8,128)(2,1)}), bf16[1024,2048]{1,0:T(8,128)(2,1)}) %all-gather.11.cloned.1.call-update) | async-done | bytes 4194320 | tf_op jit(solution)/shard_map/all_gather | solution.py:164
  360.1 4.2 gather_fusion
  364.3 111.6 %all-gather.13.cloned.1.call-done = bf16[2048,5280]{1,0:T(8,128)(2,1)} async-done(((bf16[128,5280]{1,0:T(8,128)(2,1)}), bf16[2048,5280]{1,0:T(8,128)(2,1)}) %all-gather.13.cloned.1.call-update) | async-done | bytes 21626896 | tf_op jit(solution)/shard_map/all_gather | solution.py:36
  475.9 4.4 fusion.35
  480.2 11.5 %fusion.31 = f32[1024,2048]{1,0:T(8,128)} fusion(bf16[2048,5280]{1,0:T(8,128)(2,1)} %all-gather.13.cloned.1.call-done, bf16[1024,2048]{1,0:T(8,128)(2,1)} %all-gather.11.cloned.1.call-done, f32[1024,352]{0,1:T(8,128)S(1)} %fusion.35), kind=kOutput, calls=%fused_computation.40 | convolution fusion | flops 2954952704 | bytes 17170432 | tf_op jit(solution)/shard_map/dot_general | solution.py:171
  491.7 4.8 fusion.5
  496.5 9.0 %fusion.23 = f32[128,2048]{1,0:T(8,128)S(1)} fusion(bf16[2048,5280]{1,0:T(8,128)(2,1)} %all-gather.13.cloned.1.call-done, f32[128,1408]{1,0:T(8,128)S(1)} %fusion.5, f32[128]{0:T(128)S(1)} %get-tuple-element.5, bf16[128,2048]{1,0:T(8,128)(2,1)S(1)} %gather_fusion, pred[128]{0:T(512)(128)(4,1)S(1)} %get-tuple-element.6), kind=kOutput, calls=%fused_computation.38 | convolution fusion | flops 1478000640 | bytes 13828736 | tf_op jit(solution)/shard_map/dot_general | solution.py:93
  505.5 8.8 %scatter_fusion.1 = f32[1024,2048]{1,0:T(8,128)} fusion(f32[1024,2048]{1,0:T(8,128)} %fusion.31, s32[128]{0:T(128)S(1)} %compare_select_fusion.8, f32[128,2048]{1,0:T(8,128)S(1)} %fusion.23), kind=kCustom, calls=%fused_computation.6 | custom fusion | flops 262144 | bytes 3146240 | tf_op jit(solution)/shard_map/scatter-add | solution.py:187
  514.3 4.0 convert_element_type.110
  518.3 57.5 %all_to_all.20 = bf16[8,128,2048]{2,1,0:T(8,128)(2,1)S(1)} all-to-all(bf16[8,128,2048]{2,1,0:T(8,128)(2,1)S(1)} %bitcast.78), channel_id=1, replica_groups=mesh['seq'=8,'fsdp'=16] {'seq'}, dimensions={0} | all-to-all | bytes 8388608 | tf_op jit(solution)/shard_map/all_to_all | solution.py:52
  (88 shorter events, 8.5 us)
Async XLA Ops:
  6.5 39.9 %all-gather.7.cloned.1.call-start = ((), (), s32[]{:S(2)}) async-start(), calls=%async_computation.3 | async-start | bytes 2820096 | tf_op jit(solution)/shard_map/all_gather | solution.py:12
  8.3 38.2 %copy-start.13 = (f32[1152]{0:T(1024)S(1)}, f32[1152]{0:T(1024)}, u32[]{:S(2)}) copy-start(f32[1152]{0:T(1024)} %param.24) | copy-start | bytes 13828
  8.3 139.8 %reduce-scatter.2.cloned.1.call-start = ((), (), s32[]{:S(2)}) async-start(), calls=%async_computation.4 | async-start | bytes 5308416 | tf_op jit(solution)/shard_map/reduce_scatter | solution.py:26
  8.3 3.8 copy-start
  59.5 165.6 %all-gather.15.cloned.1.call-start = ((), (), s32[]{:S(2)}) async-start(), calls=%async_computation.8 | async-start | bytes 5308416 | tf_op jit(solution)/shard_map/all_gather | solution.py:29
  148.1 110.9 %all-gather.9.cloned.1.call-start = ((), (), s32[]{:S(2)}) async-start(), calls=%async_computation.5 | async-start | bytes 2506752 | tf_op jit(solution)/shard_map/all_gather | solution.py:124
  148.7 8.7 %copy-start.14 = (s32[1,8]{1,0:T(1,128)S(1)}, s32[1,8]{1,0:T(1,128)}, u32[]{:S(2)}) copy-start(s32[1,8]{1,0:T(1,128)} %param.19) | copy-start | bytes 100
  148.7 8.8 %copy-start.12 = (s32[1,8]{1,0:T(1,128)S(1)}, s32[1,8]{1,0:T(1,128)}, u32[]{:S(2)}) copy-start(s32[1,8]{1,0:T(1,128)} %param.20) | copy-start | bytes 100
  237.1 21.9 %copy-start.10 = (f32[4608]{0:T(1024)S(1)}, f32[4608]{0:T(1024)}, u32[]{:S(2)}) copy-start(f32[4608]{0:T(1024)} %param.27) | copy-start | bytes 55300
  267.6 20.9 %copy-start.1 = (bf16[1,128,2048]{2,1,0:T(8,128)(2,1)S(1)}, bf16[1,128,2048]{2,1,0:T(8,128)(2,1)}, u32[]{:S(2)}) copy-start(bf16[1,128,2048]{2,1,0:T(8,128)(2,1)} %param.21) | copy-start | bytes 1572868
  270.7 17.7 %all-to-all-start = ((bf16[8,128,256]{2,1,0:T(8,128)(2,1)}), bf16[8,128,256]{2,1,0:T(8,128)(2,1)S(1)}, u32[]{:S(2)}, u32[]{:S(2)}) async-start(bf16[8,128,256]{2,1,0:T(8,128)(2,1)} %bitcast.15), calls=%async_computation.1 | async-start | bytes 1048576 | tf_op jit(solution)/shard_map/all_to_all | solution.py:148
  277.2 82.9 %all-gather.11.cloned.1.call-start = ((), (), s32[]{:S(2)}) async-start(), calls=%async_computation.6 | async-start | bytes 4718592 | tf_op jit(solution)/shard_map/all_gather | solution.py:164
  288.5 1.9 copy-start.11
  288.5 3.0 copy-start.6
  288.5 3.1 copy-start.7
  288.5 3.2 copy-start.8
  288.5 3.4 copy-start.2
  288.5 3.4 copy-start.3
  288.6 3.4 copy-start.4
  290.2 4.5 copy-start.5
  290.2 9.5 %copy-start.9 = (f32[1,1024,6]{1,0,2:T(1,128)S(1)}, f32[1,1024,6]{1,0,2:T(1,128)}, u32[]{:S(2)}) copy-start(f32[1,1024,6]{1,0,2:T(1,128)} %param.23) | copy-start | bytes 73732
  291.4 184.4 %all-gather.13.cloned.1.call-start = ((), (), s32[]{:S(2)}) async-start(), calls=%async_computation.7 | async-start | bytes 23396352 | tf_op jit(solution)/shard_map/all_gather | solution.py:36
Sparse Core Ops, SparseCore 0:
  9.0 37.3 all-gather.6
  59.6 88.4 reduce-scatter.1
  150.4 74.6 all-gather.14
  226.6 32.3 all-gather.8
  291.6 68.4 all-gather.10
  361.6 114.1 all-gather.12
where the time goes:
time: 591 us; the launch traced here: 585 us
  waiting for transfers between devices  379 us (64%)
  blocking collectives  57.5 us (10%)
  matrix products  51.2 us (9%)
  local copies, waits for them, and re-layouts  39.1 us (7%)
  other arithmetic  36.5 us (6%)
  between operations  14.1 us (2%)
  starting transfers between devices  7.09 us (1%)
    all_gather x1, waiting for transfers between devices, in_one_piece(): lax.all_gather(both, axis, axis=dim, tiled=True)  112 us
    reduce_scatter x1, waiting for transfers between devices, sum_in_two_steps(): lax.psum_scatter(rows_for(lines, lax.axis_size(axis)), axis, scatter_dime...  88.6 us
    all_gather x1, waiting for transfers between devices, sum_in_two_steps(): whole = lax.all_gather(own, axis).reshape(-1, *lines.shape[1:])  65.9 us
    all_gather x1, waiting for transfers between devices, shards(): gathered = lax.all_gather(normed_tokens, 'seq', axis=0, tiled=True)  57.9 us
    all_to_all x1, blocking collectives, sum_at_owner(): parts = lax.all_to_all(split_up(x, dim, count), axis, 0, 0, tiled=True)  57.5 us
    all_gather x1, waiting for transfers between devices, sent_together(): lax.all_gather(both, axis, axis=dim, tiled=True)  33 us
    all_gather x1, waiting for transfers between devices, shards(): lax.all_gather(proj_weight, 'fsdp', axis=0, tiled=True)  13.3 us
    dot_general x1, matrix products, shards(): lax.dot_general(hidden, vit_second, (((1,), (1,)), ((), ())), preferred_e...  13 us
  transfers between devices with their start and end apart: 7, of which 7 were waited for; matrix products, arithmetic and copies ran while one was open for 9% of the time, Pallas kernels for 0%

commit v1 on v0

--- a/solution.py
+++ b/solution.py
@@ -161,7 +161,9 @@
     )
     merged = embeds[0].at[slot_place].set(received[0], mode="drop")
     normed_tokens = rms_norm(merged.astype(jnp.float32), moe_gain).astype(jnp.bfloat16)
-    gathered = lax.all_gather(normed_tokens, "seq", axis=0, tiled=True)
+    gathered = jnp.concatenate(
+        lax.all_to_all(jnp.stack([normed_tokens] * lax.axis_size("seq")), "seq", 0, 0), axis=0
+    )
     gate_shared, up_shared, down_shared, gate_expert, up_expert, down_expert = in_one_piece(
         (shared_gate, shared_up, shared_down, expert_gate, expert_up, expert_down), "fsdp", 0, 1
     )

time: 591 us -> 541 us (0.915)
  waiting for transfers between devices: 379 us -> 323 us
    all_gather x1 -> x0, waiting for transfers between devices: 57.9 us -> none  [shards(): gathered = lax.all_gather(normed_tokens, 'seq', axis=0, tiled=True)]
    all_to_all x0 -> x1, waiting for transfers between devices: none -> 53.3 us  [shards(): lax.all_to_all(jnp.stack([normed_tokens] * lax.axis_size('seq')), 'seq',...]
    all_gather x1, waiting for transfers between devices: 112 us -> 62.9 us  [in_one_piece(): lax.all_gather(both, axis, axis=dim, tiled=True)]
  transfers between devices with their start and end apart: 7 -> 7, of which waited for: 7 -> 7; matrix products, arithmetic and copies ran while one was open for 9% -> 13% of each run, Pallas kernels for 0% -> 0%
where the time goes in v1:
time: 541 us; the launch traced here: 535 us
  waiting for transfers between devices  323 us (60%)
  blocking collectives  57.2 us (11%)
  matrix products  51.2 us (9%)
  local copies, waits for them, and re-layouts  42.3 us (8%)
  other arithmetic  35.7 us (7%)
  between operations  13.8 us (3%)
  starting transfers between devices  11.8 us (2%)
    reduce_scatter x1, waiting for transfers between devices, sum_in_two_steps(): lax.psum_scatter(rows_for(lines, lax.axis_size(axis)), axis, scatter_dime...  88.6 us
    all_gather x1, waiting for transfers between devices, in_one_piece(): lax.all_gather(both, axis, axis=dim, tiled=True)  62.9 us
    all_gather x1, waiting for transfers between devices, sum_in_two_steps(): whole = lax.all_gather(own, axis).reshape(-1, *lines.shape[1:])  62 us
    all_to_all x1, blocking collectives, sum_at_owner(): parts = lax.all_to_all(split_up(x, dim, count), axis, 0, 0, tiled=True)  57.2 us
    all_to_all x1, waiting for transfers between devices, shards(): lax.all_to_all(jnp.stack([normed_tokens] * lax.axis_size('seq')), 'seq',...  53.3 us
    all_gather x1, waiting for transfers between devices, sent_together(): lax.all_gather(both, axis, axis=dim, tiled=True)  33 us
    all_gather x1, waiting for transfers between devices, shards(): lax.all_gather(proj_weight, 'fsdp', axis=0, tiled=True)  13.3 us
    dot_general x1, matrix products, shards(): lax.dot_general(hidden, vit_second, (((1,), (1,)), ((), ())), preferred_e...  13 us
  transfers between devices with their start and end apart: 7, of which 7 were waited for; matrix products, arithmetic and copies ran while one was open for 13% of the time, Pallas kernels for 0%

profile of v1, /device:TPU:0, one launch (start us, length us, event | category | flops | bytes accessed | tf_op | source)
XLA Modules:
  0.0 535.0 jit_solution(17160019162314684586)
XLA Ops:
  6.5 1.7 pad_maximum_fusion
  8.3 3.2 convert_reduce_fusion
  12.1 1.4 multiply_reduce_fusion.1
  13.5 33.0 %all-gather.6.cloned.1.call-done = bf16[1152,1076]{1,0:T(8,128)(2,1)} async-done(((bf16[72,1076]{1,0:T(8,128)(2,1)}), bf16[1152,1076]{1,0:T(8,128)(2,1)}) %all-gather.6.cloned.1.call-update) | async-done | bytes 2479120 | tf_op jit(solution)/shard_map/all_gather | solution.py:12
  46.5 13.0 %convolution_convert_fusion = bf16[2048,1152]{1,0:T(8,128)(2,1)} fusion(bf16[1152,1076]{1,0:T(8,128)(2,1)} %all-gather.6.cloned.1.call-done, bf16[1,2048,1152]{2,1,0:T(8,128)(2,1)} %param.18, f32[1152]{0:T(1024)S(1)} %copy-done.13, f32[2048]{0:T(1024)S(1)} %add_rsqrt_fusion, f32[2048]{0:T(1024)S(1)} %broadcast_multiply_fusion), kind=kOutput, calls=%fused_computation.15 | convolution fusion | flops 5101277184 | bytes 12407296 | tf_op jit(solution)/shard_map/dot_general | solution.py:131
  59.6 88.6 %reduce-scatter.2.cloned.1.call-done = bf16[256,1152]{1,0:T(8,128)(2,1)} async-done(((bf16[2048,1152]{1,0:T(8,128)(2,1)}), bf16[256,1152]{1,0:T(8,128)(2,1)}) %reduce-scatter.2.cloned.1.call-update) | async-done | bytes 589840 | tf_op jit(solution)/shard_map/reduce_scatter | solution.py:26
  149.7 2.7 concatenate.7
  152.4 8.7 %reshape.287 = f32[512,4608]{1,0:T(8,128)} reshape(bf16[1,2048,1152]{2,1,0:T(8,128)(2,1)} %param.18) | data formatting | bytes 14155776 | tf_op jit(solution)/shard_map/convert_element_type | solution.py:126
  163.0 62.0 %all-gather.12.cloned.1.call-done = bf16[2048,1152]{1,0:T(8,128)(2,1)} async-done(((bf16[256,1152]{1,0:T(8,128)(2,1)}), bf16[2048,1152]{1,0:T(8,128)(2,1)}) %all-gather.12.cloned.1.call-update) | async-done | bytes 4718608 | tf_op jit(solution)/shard_map/all_gather | solution.py:29
  225.0 5.1 fusion
  230.8 5.8 %multiply_reduce_fusion = f32[2048]{0:T(1024)S(1)} fusion(bf16[1,2048,1152]{2,1,0:T(8,128)(2,1)} %param.18, bf16[2048,1152]{1,0:T(8,128)(2,1)} %all-gather.12.cloned.1.call-done, f32[2048]{0:T(1024)S(1)} %sub.65), kind=kLoop, calls=%fused_computation.10 | loop fusion | flops 14153728 | bytes 9453568 | tf_op jit(solution)/shard_map/reduce_sum | solution.py:58
  237.0 8.6 %reshape.288 = f32[512,4608]{1,0:T(8,128)} reshape(bf16[2048,1152]{1,0:T(8,128)(2,1)} %all-gather.12.cloned.1.call-done) | data formatting | bytes 14155776 | tf_op jit(solution)/shard_map/convert_element_type | solution.py:134
  245.7 13.3 %all-gather.8.cloned.1.call-done = bf16[4608,256]{1,0:T(8,128)(2,1)} async-done(((bf16[288,256]{1,0:T(8,128)(2,1)}), bf16[4608,256]{1,0:T(8,128)(2,1)}) %all-gather.8.cloned.1.call-update) | async-done | bytes 2359312 | tf_op jit(solution)/shard_map/all_gather | solution.py:124
  258.9 8.6 %fusion.49 = bf16[512,256]{1,0:T(8,128)(2,1)S(1)} fusion(bf16[4608,256]{1,0:T(8,128)(2,1)} %all-gather.8.cloned.1.call-done, f32[512,4608]{1,0:T(8,128)} %reshape.287, f32[512,4608]{1,0:T(8,128)} %reshape.288, f32[4608]{0:T(1024)S(1)} %copy-done.10, f32[512]{0:T(512)S(1)} %add_rsqrt_fusion.1, f32[512]{0:T(512)S(1)} %broadcast_multiply_fusion.1), kind=kOutput, calls=%fused_computation.53 | convolution fusion | flops 1219887104 | bytes 21518336 | tf_op jit(solution)/shard_map/dot_general | solution.py:138
  267.6 3.1 scatter_custom_fusion.1
  270.7 6.4 %all-to-all-start = ((bf16[8,128,256]{2,1,0:T(8,128)(2,1)}), bf16[8,128,256]{2,1,0:T(8,128)(2,1)S(1)}, u32[]{:S(2)}, u32[]{:S(2)}) async-start(bf16[8,128,256]{2,1,0:T(8,128)(2,1)} %bitcast.15), calls=%async_computation.1 | async-start | bytes 1048576 | tf_op jit(solution)/shard_map/all_to_all | solution.py:148
  277.1 2.4 scatter_custom_fusion
  279.6 9.5 %all-to-all-done = bf16[8,128,256]{2,1,0:T(8,128)(2,1)S(1)} async-done(((bf16[8,128,256]{2,1,0:T(8,128)(2,1)}), bf16[8,128,256]{2,1,0:T(8,128)(2,1)S(1)}, u32[]{:S(2)}, u32[]{:S(2)}) %all-to-all-start) | async-done | bytes 524320 | tf_op jit(solution)/shard_map/all_to_all | solution.py:148
  289.6 1.6 scatter_fusion
  291.7 2.5 stack.2
  294.2 4.8 all-to-all-start.1
  299.7 4.3 scatter_custom_fusion.3
  306.5 53.3 %all-to-all-done.1 = bf16[8,128,2048]{2,1,0:T(8,128)(2,1)} async-done(((bf16[8,128,2048]{2,1,0:T(8,128)(2,1)}), bf16[8,128,2048]{2,1,0:T(8,128)(2,1)}, u32[]{:S(2)}, u32[]{:S(2)}) %all-to-all-start.1) | async-done | bytes 4194336 | tf_op jit(solution)/shard_map/all_to_all | solution.py:165
  359.8 4.3 gather_fusion
  364.1 62.9 %all-gather.10.cloned.1.call-done = bf16[2048,5280]{1,0:T(8,128)(2,1)} async-done(((bf16[128,5280]{1,0:T(8,128)(2,1)}), bf16[2048,5280]{1,0:T(8,128)(2,1)}) %all-gather.10.cloned.1.call-update) | async-done | bytes 21626896 | tf_op jit(solution)/shard_map/all_gather | solution.py:36
  427.0 4.4 fusion.35
  431.3 11.5 %fusion.31 = f32[1024,2048]{1,0:T(8,128)} fusion(bf16[2048,5280]{1,0:T(8,128)(2,1)} %all-gather.10.cloned.1.call-done, bf16[1024,2048]{1,0:T(8,128)(2,1)} %bitcast.19, f32[1024,352]{0,1:T(8,128)S(1)} %fusion.35), kind=kOutput, calls=%fused_computation.40 | convolution fusion | flops 2954952704 | bytes 17170432 | tf_op jit(solution)/shard_map/dot_general | solution.py:173
  442.8 4.8 fusion.5
  447.6 9.0 %fusion.23 = f32[128,2048]{1,0:T(8,128)S(1)} fusion(bf16[2048,5280]{1,0:T(8,128)(2,1)} %all-gather.10.cloned.1.call-done, f32[128,1408]{1,0:T(8,128)S(1)} %fusion.5, f32[128]{0:T(128)S(1)} %get-tuple-element.5, bf16[128,2048]{1,0:T(8,128)(2,1)S(1)} %gather_fusion, pred[128]{0:T(512)(128)(4,1)S(1)} %get-tuple-element.6), kind=kOutput, calls=%fused_computation.38 | convolution fusion | flops 1478000640 | bytes 13828736 | tf_op jit(solution)/shard_map/dot_general | solution.py:93
  456.6 8.8 %scatter_fusion.1 = f32[1024,2048]{1,0:T(8,128)} fusion(f32[1024,2048]{1,0:T(8,128)} %fusion.31, s32[128]{0:T(128)S(1)} %compare_select_fusion.8, f32[128,2048]{1,0:T(8,128)S(1)} %fusion.23), kind=kCustom, calls=%fused_computation.6 | custom fusion | flops 262144 | bytes 3146240 | tf_op jit(solution)/shard_map/scatter-add | solution.py:189
  465.4 4.0 convert_element_type.110
  469.4 57.2 %all_to_all.25 = bf16[8,128,2048]{2,1,0:T(8,128)(2,1)S(1)} all-to-all(bf16[8,128,2048]{2,1,0:T(8,128)(2,1)S(1)} %bitcast.75), channel_id=1, replica_groups=mesh['seq'=8,'fsdp'=16] {'seq'}, dimensions={0} | all-to-all | bytes 8388608 | tf_op jit(solution)/shard_map/all_to_all | solution.py:52
  (89 shorter events, 10.8 us)
Async XLA Ops:
  6.5 39.9 %all-gather.6.cloned.1.call-start = ((), (), s32[]{:S(2)}) async-start(), calls=%async_computation.4 | async-start | bytes 2820096 | tf_op jit(solution)/shard_map/all_gather | solution.py:12
  8.3 38.2 %copy-start.13 = (f32[1152]{0:T(1024)S(1)}, f32[1152]{0:T(1024)}, u32[]{:S(2)}) copy-start(f32[1152]{0:T(1024)} %param.24) | copy-start | bytes 13828
  8.3 139.8 %reduce-scatter.2.cloned.1.call-start = ((), (), s32[]{:S(2)}) async-start(), calls=%async_computation.5 | async-start | bytes 5308416 | tf_op jit(solution)/shard_map/reduce_scatter | solution.py:26
  8.3 3.8 copy-start
  59.4 89.8 %copy-start.6 = (bf16[128,352]{0,1:T(8,128)(2,1)S(1)}, bf16[128,352]{0,1:T(8,128)(2,1)}, u32[]{:S(2)}) copy-start(bf16[128,352]{0,1:T(8,128)(2,1)} %param.30) | copy-start | bytes 270340
  59.4 89.9 %copy-start.7 = (bf16[128,352]{0,1:T(8,128)(2,1)S(1)}, bf16[128,352]{0,1:T(8,128)(2,1)}, u32[]{:S(2)}) copy-start(bf16[128,352]{0,1:T(8,128)(2,1)} %param.31) | copy-start | bytes 270340
  59.4 90.1 %copy-start.8 = (bf16[128,352]{0,1:T(8,128)(2,1)S(1)}, bf16[128,352]{0,1:T(8,128)(2,1)}, u32[]{:S(2)}) copy-start(bf16[128,352]{0,1:T(8,128)(2,1)} %param.32) | copy-start | bytes 270340
  59.4 90.2 %copy-start.2 = (bf16[128,1,1408]{2,0,1:T(8,128)(2,1)S(1)}, bf16[128,1,1408]{2,0,1:T(8,128)(2,1)}, u32[]{:S(2)}) copy-start(bf16[128,1,1408]{2,0,1:T(8,128)(2,1)} %param.33) | copy-start | bytes 1081348
  59.5 90.2 %copy-start.3 = (bf16[128,1,1408]{2,0,1:T(8,128)(2,1)S(1)}, bf16[128,1,1408]{2,0,1:T(8,128)(2,1)}, u32[]{:S(2)}) copy-start(bf16[128,1,1408]{2,0,1:T(8,128)(2,1)} %param.34) | copy-start | bytes 1081348
  59.5 90.2 %copy-start.4 = (bf16[128,1,1408]{2,0,1:T(8,128)(2,1)S(1)}, bf16[128,1,1408]{2,0,1:T(8,128)(2,1)}, u32[]{:S(2)}) copy-start(bf16[128,1,1408]{2,0,1:T(8,128)(2,1)} %param.35) | copy-start | bytes 1081348
  59.5 165.5 %all-gather.12.cloned.1.call-start = ((), (), s32[]{:S(2)}) async-start(), calls=%async_computation.8 | async-start | bytes 5308416 | tf_op jit(solution)/shard_map/all_gather | solution.py:29
  148.1 110.8 %all-gather.8.cloned.1.call-start = ((), (), s32[]{:S(2)}) async-start(), calls=%async_computation.6 | async-start | bytes 2506752 | tf_op jit(solution)/shard_map/all_gather | solution.py:124
  148.7 278.3 %all-gather.10.cloned.1.call-start = ((), (), s32[]{:S(2)}) async-start(), calls=%async_computation.7 | async-start | bytes 23396352 | tf_op jit(solution)/shard_map/all_gather | solution.py:36
  152.4 8.7 %copy-start.14 = (s32[1,8]{1,0:T(1,128)S(1)}, s32[1,8]{1,0:T(1,128)}, u32[]{:S(2)}) copy-start(s32[1,8]{1,0:T(1,128)} %param.19) | copy-start | bytes 100
  152.4 8.9 %copy-start.12 = (s32[1,8]{1,0:T(1,128)S(1)}, s32[1,8]{1,0:T(1,128)}, u32[]{:S(2)}) copy-start(s32[1,8]{1,0:T(1,128)} %param.20) | copy-start | bytes 100
  237.0 21.9 %copy-start.10 = (f32[4608]{0:T(1024)S(1)}, f32[4608]{0:T(1024)}, u32[]{:S(2)}) copy-start(f32[4608]{0:T(1024)} %param.27) | copy-start | bytes 55300
  267.6 22.1 %copy-start.1 = (bf16[1,128,2048]{2,1,0:T(8,128)(2,1)S(1)}, bf16[1,128,2048]{2,1,0:T(8,128)(2,1)}, u32[]{:S(2)}) copy-start(bf16[1,128,2048]{2,1,0:T(8,128)(2,1)} %param.21) | copy-start | bytes 1572868
  270.7 18.4 %all-to-all-start = ((bf16[8,128,256]{2,1,0:T(8,128)(2,1)}), bf16[8,128,256]{2,1,0:T(8,128)(2,1)S(1)}, u32[]{:S(2)}, u32[]{:S(2)}) async-start(bf16[8,128,256]{2,1,0:T(8,128)(2,1)} %bitcast.15), calls=%async_computation.1 | async-start | bytes 1048576 | tf_op jit(solution)/shard_map/all_to_all | solution.py:148
  289.6 1.8 copy-start.11
  294.2 4.8 copy-start.5
  294.2 9.8 %copy-start.9 = (f32[1,1024,6]{1,0,2:T(1,128)S(1)}, f32[1,1024,6]{1,0,2:T(1,128)}, u32[]{:S(2)}) copy-start(f32[1,1024,6]{1,0,2:T(1,128)} %param.23) | copy-start | bytes 73732
  294.2 65.6 %all-to-all-start.1 = ((bf16[8,128,2048]{2,1,0:T(8,128)(2,1)}), bf16[8,128,2048]{2,1,0:T(8,128)(2,1)}, u32[]{:S(2)}, u32[]{:S(2)}) async-start(bf16[8,128,2048]{2,1,0:T(8,128)(2,1)} %stack.2), calls=%async_computation.2 | async-start | bytes 8388608 | tf_op jit(solution)/shard_map/all_to_all | solution.py:165
Sparse Core Ops, SparseCore 0:
  9.0 37.3 all-gather.5
  59.6 88.4 reduce-scatter.1
  150.4 74.5 all-gather.11
  226.6 32.3 all-gather.7
  260.5 166.4 all-gather.9
